TPU v7x, 128 devices: a whole 4x4x4 slice. The times are simulated.
128 devices in a mesh: ctx: 16 (over y, z_lo, core), dp: 8 (over z_hi, x).
Axes of the slice: x: 4, y: 4, z: 4 (z_hi: 2, z_lo: 2; z = z_hi * 2 + z_lo), core: 2. Of those that a mesh axis runs over, the one named last changes fastest.
Arguments:
- query_rows: bfloat16 [8, 2048, 1024], P('dp', 'ctx'), may hold values from -6 to 6
- key_rows: bfloat16 [8, 2048, 1024], P('dp', 'ctx'), may hold values from -6 to 6
- value_rows: bfloat16 [8, 2048, 1024], P('dp', 'ctx'), may hold values from -6 to 6
- block_lists: int32 [8, 16, 4], P('dp'), may hold values from 0 to 15, as said below
- block_lengths: int32 [8, 16], P('dp'), may hold values from 2 to 128, as said below
- out_weight: bfloat16 [1024, 2048], replicated, may hold values from -0.125 to 0.125
- expert_input: bfloat16 [8, 2048, 2048], P('dp', 'ctx'), may hold values from -6 to 6
- layer_grad: bfloat16 [8, 2048, 2048], P('dp', 'ctx'), may hold values from -1.5 to 1.5
- route_experts: int32 [8, 2048, 6], P('dp', 'ctx'), may hold values from 0 to 15, all different within a row; in each aligned block of 128 rows (0 to 127, 128 to 255, ..., all dimensions but the last counted through in order) at most 64 rows name the same one
- route_weight: float32 [8, 2048, 6], P('dp', 'ctx'), may hold values from 0.02 to 0.4
- gate_weight: bfloat16 [16, 2048, 704], P('ctx'), may hold values from -0.125 to 0.125
- up_weight: bfloat16 [16, 2048, 704], P('ctx'), may hold values from -0.125 to 0.125
- down_weight: bfloat16 [16, 2048, 704], P('ctx'), may hold values from -0.21875 to 0.21875
Outputs:
- query_grad: bfloat16 [8, 2048, 1024], P('dp', 'ctx')
- key_grad: bfloat16 [8, 2048, 1024], P('dp', 'ctx')
- value_grad: bfloat16 [8, 2048, 1024], P('dp', 'ctx')
- gate_grad: float32 [16, 2048, 704], P('ctx', 'dp')
- up_grad: float32 [16, 2048, 704], P('ctx', 'dp')
- down_grad: float32 [16, 2048, 704], P('ctx', 'dp')
Inputs may be any that keep to these rules, and one draw needn't show every extreme that they name: `block_lists`: entry 0 of row i of a sequence's lists is i; every entry of row i lies in 0 to i. `block_lengths`: every sequence has a block of full length 128. `route_experts`: each token names 6 different experts. Among the 128 tokens of one device, no expert is named by more than 64 tokens.
All inputs are finite; a program needn't handle non-finite values.
Results may differ from a plain program's by a relative error of at most 0.012.
The roundings to bfloat16 on the way count: a program that leaves them out, or rounds other values in their place, can miss the bound.
Values may be sent and summed in bfloat16 or wider, within the bound.
No kernel may reach another device: no remote copies, remote signals or barrier semaphores. Data moves between devices by JAX's collectives and lax.ppermute only.
A program may use at most 192 MiB of HBM per device.

v0:
```python
import math
import jax
import jax.numpy as jnp
from jax import lax
from jax.sharding import PartitionSpec as P

HEADS = 8
HD = 128
TOPK = 6
EXP_DEV = 1
BLK = 128
NSEL = 4


def route_coefficients(chosen, rweights, expert_list):
    matches = chosen[:, :, None] == expert_list[None, None, :]
    return jnp.sum(jnp.where(matches, rweights[:, :, None], 0.0), axis=1)


def slot_rows(tokens, grad_rows, coef_rows, capacity):
    present = coef_rows > 0.0
    rank_rows = jnp.cumsum(present.astype(jnp.int32), axis=0) - 1
    slot_ids = jnp.arange(capacity, dtype=jnp.int32)
    chosen_slot = present.T[:, None, :] & (rank_rows.T[:, None, :] == slot_ids[None, :, None])
    onehot = chosen_slot.astype(jnp.bfloat16)
    picked = jnp.einsum("ecs,sd->ecd", onehot, tokens, preferred_element_type=jnp.float32).astype(
        jnp.bfloat16
    )
    picked_grad = jnp.einsum("ecs,sd->ecd", onehot, grad_rows, preferred_element_type=jnp.float32)
    slot_coef = jnp.sum(jnp.where(chosen_slot, coef_rows.T[:, None, :], 0.0), axis=2)
    scaled = (slot_coef[:, :, None] * picked_grad).astype(jnp.bfloat16)
    return (picked, scaled)


def per_device(
    query_rows,
    key_rows,
    value_rows,
    block_lists,
    block_lengths,
    out_weight,
    expert_input,
    layer_grad,
    route_experts,
    route_weight,
    gate_weight,
    up_weight,
    down_weight,
):
    ctx_count = lax.axis_size("ctx")
    my_index = lax.axis_index("ctx")
    local_rows = query_rows.shape[1]
    seq_len = local_rows * ctx_count
    block_total = seq_len // BLK
    row_width = HEADS * HD
    inv_root = 1.0 / math.sqrt(HD)
    my_start = my_index * local_rows
    queries = query_rows[0]
    out_grad = jnp.einsum(
        "sd,wd->sw", layer_grad[0], out_weight, preferred_element_type=jnp.float32
    ).astype(jnp.bfloat16)
    whole_keys, whole_values = (
        lax.all_gather(key_rows[0], "ctx", axis=0, tiled=True),
        lax.all_gather(value_rows[0], "ctx", axis=0, tiled=True),
    )
    lengths_row = block_lengths[0]
    query_blocks = local_rows // BLK
    lists_here = lax.dynamic_slice_in_dim(block_lists[0], my_index * query_blocks, query_blocks, 0)
    entry_ids = jnp.arange(NSEL, dtype=jnp.int32)
    repeated = jnp.any(
        (lists_here[:, :, None] == lists_here[:, None, :])
        & (entry_ids[None, None, :] < entry_ids[None, :, None]),
        axis=2,
    )
    key_tiles = whole_keys.reshape(block_total, BLK, HEADS, HD)[lists_here].reshape(
        query_blocks, NSEL * BLK, HEADS, HD
    )
    value_tiles = whole_values.reshape(block_total, BLK, HEADS, HD)[lists_here].reshape(
        query_blocks, NSEL * BLK, HEADS, HD
    )
    offsets = jnp.arange(BLK, dtype=jnp.int32)
    key_pos = (lists_here[:, :, None] * BLK + offsets[None, None, :]).reshape(
        query_blocks, NSEL * BLK
    )
    present = (
        (offsets[None, None, :] < lengths_row[lists_here][:, :, None])
        & jnp.logical_not(repeated)[:, :, None]
    ).reshape(query_blocks, NSEL * BLK)
    query_pos = my_start + (
        jnp.arange(query_blocks, dtype=jnp.int32)[:, None] * BLK + offsets[None, :]
    )
    allowed = present[:, None, :] & (query_pos[:, :, None] >= key_pos[:, None, :])
    query_heads = queries.reshape(query_blocks, BLK, HEADS, HD)
    grad_heads = out_grad.reshape(query_blocks, BLK, HEADS, HD)
    raw_scores = (
        jnp.einsum("bqhd,bkhd->bhqk", query_heads, key_tiles, preferred_element_type=jnp.float32)
        * inv_root
    )
    scores = jnp.where(allowed[:, None], raw_scores, -jnp.inf)
    row_max = jnp.max(scores, axis=3)
    log_total = row_max + jnp.log(jnp.sum(jnp.exp(scores - row_max[..., None]), axis=3))
    prob_full = jnp.exp(scores - log_total[..., None])
    prob_low = prob_full.astype(jnp.bfloat16)
    head_output = jnp.einsum(
        "bhqk,bkhd->bqhd", prob_low, value_tiles, preferred_element_type=jnp.float32
    )
    row_delta = jnp.sum(head_output * grad_heads.astype(jnp.float32), axis=3)
    prob_grad = jnp.einsum(
        "bqhd,bkhd->bhqk", grad_heads, value_tiles, preferred_element_type=jnp.float32
    )
    dscore = (prob_full * (prob_grad - jnp.swapaxes(row_delta, 1, 2)[..., None])).astype(
        jnp.bfloat16
    )
    query_total = jnp.einsum(
        "bhqk,bkhd->bqhd", dscore, key_tiles, preferred_element_type=jnp.float32
    )
    query_grad = (query_total * inv_root).reshape(1, local_rows, row_width).astype(jnp.bfloat16)
    key_term = (
        jnp.einsum("bhqk,bqhd->bkhd", dscore, query_heads, preferred_element_type=jnp.float32)
        * inv_root
    )
    value_term = jnp.einsum(
        "bhqk,bqhd->bkhd", prob_low, grad_heads, preferred_element_type=jnp.float32
    )
    flat_lists = lists_here.reshape(query_blocks * NSEL)
    empty_rows = jnp.zeros((block_total, BLK, row_width), jnp.float32)
    key_part = empty_rows.at[flat_lists].add(key_term.reshape(query_blocks * NSEL, BLK, row_width))
    value_part = empty_rows.at[flat_lists].add(
        value_term.reshape(query_blocks * NSEL, BLK, row_width)
    )
    key_sum, value_sum = (
        lax.psum_scatter(
            key_part.reshape(seq_len, row_width).astype(jnp.bfloat16),
            "ctx",
            scatter_dimension=0,
            tiled=True,
        ).astype(jnp.float32),
        lax.psum_scatter(
            value_part.reshape(seq_len, row_width).astype(jnp.bfloat16),
            "ctx",
            scatter_dimension=0,
            tiled=True,
        ).astype(jnp.float32),
    )
    key_grad = key_sum.reshape(1, local_rows, row_width).astype(jnp.bfloat16)
    value_grad = value_sum.reshape(1, local_rows, row_width).astype(jnp.bfloat16)
    tokens_here = expert_input[0]
    grads_here = layer_grad[0]
    expert_count = EXP_DEV * ctx_count
    capacity = min(local_rows, local_rows * TOPK * 4 // (3 * expert_count))
    all_experts = jnp.arange(expert_count, dtype=jnp.int32)
    coef_here = route_coefficients(route_experts[0], route_weight[0], all_experts)
    picked, scaled = slot_rows(tokens_here, grads_here, coef_here, capacity)
    rows_in, grads_in = (
        lax.all_to_all(picked, "ctx", split_axis=0, concat_axis=1, tiled=True),
        lax.all_to_all(scaled, "ctx", split_axis=0, concat_axis=1, tiled=True),
    )
    gate_pre = jnp.einsum("erd,edf->erf", rows_in, gate_weight, preferred_element_type=jnp.float32)
    up_pre = jnp.einsum("erd,edf->erf", rows_in, up_weight, preferred_element_type=jnp.float32)
    gate_sig = jax.nn.sigmoid(gate_pre)
    gate_act = gate_pre * gate_sig
    hidden = (gate_act * up_pre).astype(jnp.bfloat16)
    down_part = jnp.einsum("erd,erf->edf", grads_in, hidden, preferred_element_type=jnp.float32)
    hidden_grad = jnp.einsum(
        "erd,edf->erf", grads_in, down_weight, preferred_element_type=jnp.float32
    )
    gate_delta = (hidden_grad * up_pre * gate_sig * (1.0 + gate_pre * (1.0 - gate_sig))).astype(
        jnp.bfloat16
    )
    up_delta = (hidden_grad * gate_act).astype(jnp.bfloat16)
    gate_part = jnp.einsum("erd,erf->edf", rows_in, gate_delta, preferred_element_type=jnp.float32)
    up_part = jnp.einsum("erd,erf->edf", rows_in, up_delta, preferred_element_type=jnp.float32)
    gate_grad, up_grad, down_grad = (
        lax.psum_scatter(
            gate_part.astype(jnp.bfloat16), "dp", scatter_dimension=1, tiled=True
        ).astype(jnp.float32),
        lax.psum_scatter(
            up_part.astype(jnp.bfloat16), "dp", scatter_dimension=1, tiled=True
        ).astype(jnp.float32),
        lax.psum_scatter(
            down_part.astype(jnp.bfloat16), "dp", scatter_dimension=1, tiled=True
        ).astype(jnp.float32),
    )
    return (query_grad, key_grad, value_grad, gate_grad, up_grad, down_grad)


def solution(mesh):
    in_specs = (
        P("dp", "ctx", None),
        P("dp", "ctx", None),
        P("dp", "ctx", None),
        P("dp", None, None),
        P("dp", None),
        P(),
        P("dp", "ctx", None),
        P("dp", "ctx", None),
        P("dp", "ctx", None),
        P("dp", "ctx", None),
        P("ctx", None, None),
        P("ctx", None, None),
        P("ctx", None, None),
    )
    out_specs = (
        P("dp", "ctx", None),
        P("dp", "ctx", None),
        P("dp", "ctx", None),
        P("ctx", "dp", None),
        P("ctx", "dp", None),
        P("ctx", "dp", None),
    )
    return jax.shard_map(
        per_device, mesh=mesh, in_specs=in_specs, out_specs=out_specs, check_vma=False
    )
```

profile of v0, /device:TPU:2, one launch (start us, length us, event | category | flops | bytes accessed | tf_op | source)
XLA Modules:
  0.0 577.1 jit_solution(10872713448097858192)
XLA Ops:
  8.1 0.7 all-gather.5.cloned.1.call-update
  8.7 0.8 copy.104
  9.6 0.7 copy.105
  10.6 4.2 convolution_convert_fusion
  14.8 6.1 %all-to-all-start = ((bf16[16,64,2048]{2,1,0:T(8,128)(2,1)}), bf16[16,64,2048]{2,1,0:T(8,128)(2,1)}, u32[]{:S(2)}, u32[]{:S(2)}) async-start(bf16[16,64,2048]{2,1,0:T(8,128)(2,1)} %convolution_convert_fusion), calls=%async_computation.2 | async-start | bytes 8388608 | tf_op jit(solution)/shard_map/all_to_all | solution.py:155
  21.0 0.7 all-gather.7.cloned.1.call-update
  22.0 3.3 multiply_convert_fusion
  25.3 69.5 %all-to-all-done = bf16[16,64,2048]{2,1,0:T(8,128)(2,1)} async-done(((bf16[16,64,2048]{2,1,0:T(8,128)(2,1)}), bf16[16,64,2048]{2,1,0:T(8,128)(2,1)}, u32[]{:S(2)}, u32[]{:S(2)}) %all-to-all-start) | async-done | bytes 4194336 | tf_op jit(solution)/shard_map/all_to_all | solution.py:155
  94.7 7.8 %all-to-all-start.1 = ((bf16[16,64,2048]{2,1,0:T(8,128)(2,1)}), bf16[16,64,2048]{2,1,0:T(8,128)(2,1)}, u32[]{:S(2)}, u32[]{:S(2)}) async-start(bf16[16,64,2048]{2,1,0:T(8,128)(2,1)} %multiply_convert_fusion), calls=%async_computation.3 | async-start | bytes 8388608 | tf_op jit(solution)/shard_map/all_to_all | solution.py:156
  102.8 7.1 %fusion.3 = f32[1024,704]{0,1:T(8,128)} fusion(bf16[1024,2048]{1,0:T(8,128)(2,1)} %bitcast.33, bf16[1,2048,704]{1,2,0:T(8,128)(2,1)S(1)} %copy-done), kind=kOutput, calls=%fused_computation.13 | convolution fusion | flops 2952790016 | bytes 9961472 | tf_op jit(solution)/shard_map/erd,edf->erf/dot_general | solution.py:158
  109.9 7.1 %fusion.5 = f32[1024,704]{0,1:T(8,128)} fusion(bf16[1024,2048]{1,0:T(8,128)(2,1)} %bitcast.33, bf16[1,2048,704]{1,2,0:T(8,128)(2,1)S(1)} %copy-done.8), kind=kOutput, calls=%fused_computation.15 | convolution fusion | flops 2952790016 | bytes 9961472 | tf_op jit(solution)/shard_map/erd,edf->erf/dot_general | solution.py:159
  117.1 45.9 %all-to-all-done.1 = bf16[16,64,2048]{2,1,0:T(8,128)(2,1)} async-done(((bf16[16,64,2048]{2,1,0:T(8,128)(2,1)}), bf16[16,64,2048]{2,1,0:T(8,128)(2,1)}, u32[]{:S(2)}, u32[]{:S(2)}) %all-to-all-start.1) | async-done | bytes 4194336 | tf_op jit(solution)/shard_map/all_to_all | solution.py:156
  163.0 5.2 fusion.7
  168.2 1.5 copy-done.13
  169.7 7.4 %fusion = bf16[1,2048,704]{1,2,0:T(8,128)(2,1)} fusion(bf16[1024,2048]{1,0:T(8,128)(2,1)} %bitcast.33, f32[1024,704]{0,1:T(8,128)S(1)} %copy-done.10, f32[1024,704]{0,1:T(8,128)S(1)} %fusion.7, f32[1024,704]{0,1:T(8,128)S(1)} %copy-done.12), kind=kOutput, calls=%fused_computation.10 | convolution fusion | flops 2961440768 | bytes 15728640 | tf_op jit(solution)/shard_map/erd,erf->edf/dot_general | solution.py:171
  177.2 1.8 copy-done.11
  179.0 7.9 %fusion.1 = bf16[1,2048,704]{1,2,0:T(8,128)(2,1)} fusion(bf16[1024,2048]{1,0:T(8,128)(2,1)} %bitcast.33, f32[1024,704]{0,1:T(8,128)} %copy-done.13, f32[1024,704]{0,1:T(8,128)S(1)} %copy-done.11), kind=kOutput, calls=%fused_computation.11 | convolution fusion | flops 2958557184 | bytes 12845056 | tf_op jit(solution)/shard_map/erd,erf->edf/dot_general | solution.py:172
  187.0 7.9 %fusion.2 = bf16[1,2048,704]{1,2,0:T(8,128)(2,1)} fusion(bf16[1024,2048]{1,0:T(8,128)(2,1)} %bitcast.35, f32[1024,704]{0,1:T(8,128)} %fusion.5, f32[1024,704]{0,1:T(8,128)S(1)} %copy-done.11), kind=kOutput, calls=%fused_computation.12 | convolution fusion | flops 2958557184 | bytes 12845056 | tf_op jit(solution)/shard_map/erd,erf->edf/dot_general | solution.py:163
  195.3 3.9 convolution_convert_fusion.4
  201.1 5.3 copy.93
  206.5 3.0 gather_fusion
  209.5 1.5 copy.83
  211.0 5.4 copy.95
  216.4 3.0 gather_fusion.2
  219.4 1.5 copy.78
  220.9 1.9 fusion.39
  223.7 0.7 multiply_convert_fusion.4
  224.4 1.0 copy-done.4
  225.8 2.5 copy.70
  228.3 2.8 reshape.550
  231.1 4.3 broadcast_in_dim.38.clone
  235.5 4.5 scatter_fusion
  240.0 6.1 %convert_element_type.125 = bf16[16,128,1024]{2,1,0:T(8,128)(2,1)} convert(f32[16,128,1024]{2,1,0:T(8,128)} %scatter_fusion) | non-fusion elementwise | flops 2097152 | bytes 12582912 | tf_op jit(solution)/shard_map/convert_element_type | solution.py:133
  246.4 1.8 convolution_bitcast_fusion
  248.2 2.9 reshape.558
  251.1 1.9 copy.73
  253.0 4.4 broadcast_in_dim.38.clone.1
  257.4 4.1 scatter_fusion.1
  261.5 6.1 %convert_element_type.128 = bf16[16,128,1024]{2,1,0:T(8,128)(2,1)} convert(f32[16,128,1024]{2,1,0:T(8,128)} %scatter_fusion.1) | non-fusion elementwise | flops 2097152 | bytes 12582912 | tf_op jit(solution)/shard_map/convert_element_type | solution.py:139
  267.6 2.1 fusion.13
  269.7 0.9 copy.76
  270.6 1.9 convert_element_type.137
  272.5 75.3 %reduce-scatter.12.cloned.1.call-done = bf16[1,256,704]{1,2,0:T(8,128)(2,1)} async-done(((bf16[1,2048,704]{1,2,0:T(8,128)(2,1)}), bf16[1,256,704]{1,2,0:T(8,128)(2,1)}) %reduce-scatter.12.cloned.1.call-update) | async-done | bytes 360464 | tf_op jit(solution)/shard_map/reduce_scatter | solution.py:177
  347.8 1.9 convert_element_type.141
  349.7 79.9 %reduce-scatter.14.cloned.1.call-done = bf16[1,256,704]{1,2,0:T(8,128)(2,1)} async-done(((bf16[1,2048,704]{1,2,0:T(8,128)(2,1)}), bf16[1,256,704]{1,2,0:T(8,128)(2,1)}) %reduce-scatter.14.cloned.1.call-update) | async-done | bytes 360464 | tf_op jit(solution)/shard_map/reduce_scatter | solution.py:180
  429.6 1.9 convert_element_type.145
  431.5 68.1 %reduce-scatter.6.cloned.1.call-done = bf16[128,1024]{1,0:T(8,128)(2,1)} async-done(((bf16[2048,1024]{1,0:T(8,128)(2,1)}), bf16[128,1024]{1,0:T(8,128)(2,1)}) %reduce-scatter.6.cloned.1.call-update) | async-done | bytes 262160 | tf_op jit(solution)/shard_map/reduce_scatter | solution.py:132
  499.6 69.9 %reduce-scatter.8.cloned.1.call-done = bf16[128,1024]{1,0:T(8,128)(2,1)} async-done(((bf16[2048,1024]{1,0:T(8,128)(2,1)}), bf16[128,1024]{1,0:T(8,128)(2,1)}) %reduce-scatter.8.cloned.1.call-update) | async-done | bytes 262160 | tf_op jit(solution)/shard_map/reduce_scatter | solution.py:138
  (69 shorter events, 4.8 us)
Async XLA Ops:
  8.0 94.8 %copy-start = (bf16[1,2048,704]{1,2,0:T(8,128)(2,1)S(1)}, bf16[1,2048,704]{1,2,0:T(8,128)(2,1)}, u32[]{:S(2)}) copy-start(bf16[1,2048,704]{1,2,0:T(8,128)(2,1)} %param.23) | copy-start | bytes 8650756
  8.0 193.1 %all-gather.5.cloned.1.call-start = ((), (), s32[]{:S(2)}) async-start(), calls=%async_computation.12 | async-start | bytes 4456448 | tf_op jit(solution)/shard_map/all_gather | solution.py:63
  14.8 7.1 %copy-start.5 = (bf16[1,128,2048]{2,1,0:T(8,128)(2,1)S(1)}, bf16[1,128,2048]{2,1,0:T(8,128)(2,1)}, u32[]{:S(2)}) copy-start(bf16[1,128,2048]{2,1,0:T(8,128)(2,1)} %param.20) | copy-start | bytes 1572868
  14.8 79.9 %all-to-all-start = ((bf16[16,64,2048]{2,1,0:T(8,128)(2,1)}), bf16[16,64,2048]{2,1,0:T(8,128)(2,1)}, u32[]{:S(2)}, u32[]{:S(2)}) async-start(bf16[16,64,2048]{2,1,0:T(8,128)(2,1)} %convolution_convert_fusion), calls=%async_computation.2 | async-start | bytes 8388608 | tf_op jit(solution)/shard_map/all_to_all | solution.py:155
  21.0 190.0 %all-gather.7.cloned.1.call-start = ((), (), s32[]{:S(2)}) async-start(), calls=%async_computation.13 | async-start | bytes 4456448 | tf_op jit(solution)/shard_map/all_gather | solution.py:64
  94.7 68.3 %all-to-all-start.1 = ((bf16[16,64,2048]{2,1,0:T(8,128)(2,1)}), bf16[16,64,2048]{2,1,0:T(8,128)(2,1)}, u32[]{:S(2)}, u32[]{:S(2)}) async-start(bf16[16,64,2048]{2,1,0:T(8,128)(2,1)} %multiply_convert_fusion), calls=%async_computation.3 | async-start | bytes 8388608 | tf_op jit(solution)/shard_map/all_to_all | solution.py:156
  102.6 168.0 %reduce-scatter.10.cloned.1.call-start = ((), (), s32[]{:S(2)}) async-start(), calls=%async_computation.9 | async-start | bytes 3244032 | tf_op jit(solution)/shard_map/reduce_scatter | solution.py:174
  102.8 7.1 %copy-start.8 = (bf16[1,2048,704]{1,2,0:T(8,128)(2,1)S(1)}, bf16[1,2048,704]{1,2,0:T(8,128)(2,1)}, u32[]{:S(2)}) copy-start(bf16[1,2048,704]{1,2,0:T(8,128)(2,1)} %param.24) | copy-start | bytes 8650756
  109.9 53.1 %copy-start.9 = (bf16[1,2048,704]{1,2,0:T(8,128)(2,1)S(1)}, bf16[1,2048,704]{1,2,0:T(8,128)(2,1)}, u32[]{:S(2)}) copy-start(bf16[1,2048,704]{1,2,0:T(8,128)(2,1)} %param.25) | copy-start | bytes 8650756
  163.0 6.7 %copy-start.10 = (f32[1024,704]{0,1:T(8,128)S(1)}, f32[1024,704]{0,1:T(8,128)}, u32[]{:S(2)}) copy-start(f32[1024,704]{0,1:T(8,128)} %fusion.3) | copy-start | bytes 8650756
  163.0 6.7 %copy-start.12 = (f32[1024,704]{0,1:T(8,128)S(1)}, f32[1024,704]{0,1:T(8,128)}, u32[]{:S(2)}) copy-start(f32[1024,704]{0,1:T(8,128)} %fusion.5) | copy-start | bytes 8650756
  168.2 1.5 copy-start.13
  177.1 1.9 copy-start.11
  177.2 170.6 %reduce-scatter.12.cloned.1.call-start = ((), (), s32[]{:S(2)}) async-start(), calls=%async_computation.10 | async-start | bytes 3244032 | tf_op jit(solution)/shard_map/reduce_scatter | solution.py:177
  187.0 242.6 %reduce-scatter.14.cloned.1.call-start = ((), (), s32[]{:S(2)}) async-start(), calls=%async_computation.11 | async-start | bytes 3244032 | tf_op jit(solution)/shard_map/reduce_scatter | solution.py:180
  194.9 304.6 %reduce-scatter.6.cloned.1.call-start = ((), (), s32[]{:S(2)}) async-start(), calls=%async_computation.7 | async-start | bytes 4456448 | tf_op jit(solution)/shard_map/reduce_scatter | solution.py:132
  195.2 4.3 copy-start.6
  195.2 4.4 copy-start.7
  195.2 4.8 copy-start.2
  220.9 2.2 copy-start.3
  224.4 1.0 copy-start.4
  246.1 323.4 %reduce-scatter.8.cloned.1.call-start = ((), (), s32[]{:S(2)}) async-start(), calls=%async_computation.8 | async-start | bytes 4456448 | tf_op jit(solution)/shard_map/reduce_scatter | solution.py:138
  267.6 301.9 %copy-start.1 = (bf16[1,2048,704]{1,2,0:T(8,128)(2,1)S(1)}, bf16[1,2048,704]{1,2,0:T(8,128)(2,1)}, u32[]{:S(2)}) copy-start(bf16[1,2048,704]{1,2,0:T(8,128)(2,1)} %param.23) | copy-start | bytes 8650756
Sparse Core Ops, SparseCore 0:
  10.5 81.0 all-gather.4
  93.3 89.8 all-gather.6
Sparse Core Ops, SparseCore 1:
  177.2 88.6 reduce-scatter.9
  269.6 78.1 reduce-scatter.11
  351.5 78.0 reduce-scatter.13
  432.6 67.0 reduce-scatter.5
  502.6 66.9 reduce-scatter.7
where the time goes:
time: 578 us; the launch traced here: 577 us
  waiting for transfers between devices  410 us (71%)
  matrix products  61.6 us (11%)
  local copies, waits for them, and re-layouts  46.8 us (8%)
  other arithmetic  27.7 us (5%)
  between operations  16 us (3%)
  starting transfers between devices  14.9 us (3%)
    reduce_scatter x1, waiting for transfers between devices, per_device(): lax.psum_scatter(down_part.astype(jnp.bfloat16), 'dp', scatter_dimension=...  79.9 us
    reduce_scatter x1, waiting for transfers between devices, per_device(): lax.psum_scatter(up_part.astype(jnp.bfloat16), 'dp', scatter_dimension=1,...  75.3 us
    reduce_scatter x1, waiting for transfers between devices, per_device(): lax.psum_scatter(value_part.reshape(seq_len, row_width).astype(jnp.bfloat...  69.9 us
    all_to_all x1, waiting for transfers between devices, per_device(): lax.all_to_all(picked, 'ctx', split_axis=0, concat_axis=1, tiled=True)  69.5 us
    reduce_scatter x1, waiting for transfers between devices, per_device(): lax.psum_scatter(key_part.reshape(seq_len, row_width).astype(jnp.bfloat16...  68.1 us
    all_to_all x1, waiting for transfers between devices, per_device(): lax.all_to_all(scaled, 'ctx', split_axis=0, concat_axis=1, tiled=True)  45.9 us
    unnamed x34, local copies, waits for them, and re-layouts  17.5 us
  transfers between devices with their start and end apart: 9, of which 6 were waited for; matrix products, arithmetic and copies ran while one was open for 23% of the time, Pallas kernels for 0%

commit v1 on v0

--- a/solution.py
+++ b/solution.py
@@ -152,7 +152,15 @@
     coef_here = route_coefficients(route_experts[0], route_weight[0], all_experts)
     picked, scaled = slot_rows(tokens_here, grads_here, coef_here, capacity)
     rows_in, grads_in = (
-        lax.all_to_all(picked, "ctx", split_axis=0, concat_axis=1, tiled=True),
+        jnp.concatenate(
+            jax.lax.all_to_all(
+                jnp.stack(jnp.split(picked, jax.lax.axis_size("ctx"), axis=0)),
+                "ctx",
+                split_axis=0,
+                concat_axis=0,
+            ),
+            axis=1,
+        ),
         lax.all_to_all(scaled, "ctx", split_axis=0, concat_axis=1, tiled=True),
     )
     gate_pre = jnp.einsum("erd,edf->erf", rows_in, gate_weight, preferred_element_type=jnp.float32)

time: 578 us -> 588 us (1.017)
  local copies, waits for them, and re-layouts: 46.8 us -> 56.6 us
    unnamed x34 -> x49, local copies, waits for them, and re-layouts: 17.5 us -> 26.5 us
    all_to_all x1, waiting for transfers between devices: 45.9 us -> 53.8 us  [per_device(): lax.all_to_all(scaled, 'ctx', split_axis=0, concat_axis=1, tiled=True)]
    all_to_all x1, waiting for transfers between devices: 69.5 us -> 61.8 us  [per_device(): jax.lax.all_to_all(jnp.stack(jnp.split(picked, jax.lax.axis_size('ctx'),...]
  transfers between devices with their start and end apart: 9 -> 9, of which waited for: 6 -> 6; matrix products, arithmetic and copies ran while one was open for 23% -> 24% of each run, Pallas kernels for 0% -> 0%
where the time goes in v1:
time: 588 us; the launch traced here: 587 us
  waiting for transfers between devices  410 us (70%)
  matrix products  59.4 us (10%)
  local copies, waits for them, and re-layouts  56.6 us (10%)
  other arithmetic  27.4 us (5%)
  starting transfers between devices  18.2 us (3%)
  between operations  16 us (3%)
    reduce_scatter x1, waiting for transfers between devices, per_device(): lax.psum_scatter(down_part.astype(jnp.bfloat16), 'dp', scatter_dimension=...  79.9 us
    reduce_scatter x1, waiting for transfers between devices, per_device(): lax.psum_scatter(up_part.astype(jnp.bfloat16), 'dp', scatter_dimension=1,...  74.9 us
    reduce_scatter x1, waiting for transfers between devices, per_device(): lax.psum_scatter(value_part.reshape(seq_len, row_width).astype(jnp.bfloat...  69.8 us
    reduce_scatter x1, waiting for transfers between devices, per_device(): lax.psum_scatter(key_part.reshape(seq_len, row_width).astype(jnp.bfloat16...  68 us
    all_to_all x1, waiting for transfers between devices, per_device(): jax.lax.all_to_all(jnp.stack(jnp.split(picked, jax.lax.axis_size('ctx'),...  61.8 us
    all_to_all x1, waiting for transfers between devices, per_device(): lax.all_to_all(scaled, 'ctx', split_axis=0, concat_axis=1, tiled=True)  53.8 us
    unnamed x49, local copies, waits for them, and re-layouts  26.5 us
  transfers between devices with their start and end apart: 9, of which 6 were waited for; matrix products, arithmetic and copies ran while one was open for 24% of the time, Pallas kernels for 0%

profile of v1, /device:TPU:2, one launch (start us, length us, event | category | flops | bytes accessed | tf_op | source)
XLA Modules:
  0.0 587.4 jit_solution(1197341654157299679)
XLA Ops:
  8.7 0.8 copy.104
  10.6 2.3 convolution_convert_fusion
  14.4 0.7 fusion.38
  19.4 0.7 fusion.31
  20.1 0.7 fusion.30
  22.3 0.7 fusion.27
  23.8 0.7 fusion.25
  24.5 6.1 %all-to-all-start = ((bf16[16,1,64,2048]{3,2,1,0:T(8,128)(2,1)}), bf16[16,1,64,2048]{3,2,1,0:T(8,128)(2,1)}, u32[]{:S(2)}, u32[]{:S(2)}) async-start(bf16[16,1,64,2048]{3,2,1,0:T(8,128)(2,1)} %fusion.25), calls=%async_computation.2 | async-start | bytes 8388608 | tf_op jit(solution)/shard_map/all_to_all | solution.py:156
  31.6 3.2 multiply_convert_fusion
  34.8 61.8 %all-to-all-done = bf16[16,1,64,2048]{3,2,1,0:T(8,128)(2,1)} async-done(((bf16[16,1,64,2048]{3,2,1,0:T(8,128)(2,1)}), bf16[16,1,64,2048]{3,2,1,0:T(8,128)(2,1)}, u32[]{:S(2)}, u32[]{:S(2)}) %all-to-all-start) | async-done | bytes 4194336 | tf_op jit(solution)/shard_map/all_to_all | solution.py:156
  96.6 11.1 %all-to-all-start.1 = ((bf16[16,64,2048]{2,1,0:T(8,128)(2,1)}), bf16[16,64,2048]{2,1,0:T(8,128)(2,1)}, u32[]{:S(2)}, u32[]{:S(2)}) async-start(bf16[16,64,2048]{2,1,0:T(8,128)(2,1)} %multiply_convert_fusion), calls=%async_computation.3 | async-start | bytes 8388608 | tf_op jit(solution)/shard_map/all_to_all | solution.py:164
  108.0 7.1 %fusion.3 = f32[1024,704]{0,1:T(8,128)} fusion(bf16[1024,2048]{1,0:T(8,128)(2,1)} %bitcast.49, bf16[1,2048,704]{1,2,0:T(8,128)(2,1)S(1)} %copy-done), kind=kOutput, calls=%fused_computation.13 | convolution fusion | flops 2952790016 | bytes 9961472 | tf_op jit(solution)/shard_map/erd,edf->erf/dot_general | solution.py:166
  115.1 7.2 %fusion.5 = f32[1024,704]{0,1:T(8,128)} fusion(bf16[1024,2048]{1,0:T(8,128)(2,1)} %bitcast.49, bf16[1,2048,704]{1,2,0:T(8,128)(2,1)S(1)} %copy-done.8), kind=kOutput, calls=%fused_computation.15 | convolution fusion | flops 2952790016 | bytes 9961472 | tf_op jit(solution)/shard_map/erd,edf->erf/dot_general | solution.py:167
  122.4 53.8 %all-to-all-done.1 = bf16[16,64,2048]{2,1,0:T(8,128)(2,1)} async-done(((bf16[16,64,2048]{2,1,0:T(8,128)(2,1)}), bf16[16,64,2048]{2,1,0:T(8,128)(2,1)}, u32[]{:S(2)}, u32[]{:S(2)}) %all-to-all-start.1) | async-done | bytes 4194336 | tf_op jit(solution)/shard_map/all_to_all | solution.py:164
  176.1 5.1 fusion.7
  181.3 1.6 copy-done.13
  183.0 7.5 %fusion = bf16[1,2048,704]{1,2,0:T(8,128)(2,1)} fusion(bf16[1024,2048]{1,0:T(8,128)(2,1)} %bitcast.49, f32[1024,704]{0,1:T(8,128)S(1)} %copy-done.10, f32[1024,704]{0,1:T(8,128)S(1)} %fusion.7, f32[1024,704]{0,1:T(8,128)S(1)} %copy-done.12), kind=kOutput, calls=%fused_computation.10 | convolution fusion | flops 2961440768 | bytes 15728640 | tf_op jit(solution)/shard_map/erd,erf->edf/dot_general | solution.py:179
  190.6 7.9 %fusion.1 = bf16[1,2048,704]{1,2,0:T(8,128)(2,1)} fusion(bf16[1024,2048]{1,0:T(8,128)(2,1)} %bitcast.49, f32[1024,704]{0,1:T(8,128)} %copy-done.13, f32[1024,704]{0,1:T(8,128)S(1)} %copy-done.11), kind=kOutput, calls=%fused_computation.11 | convolution fusion | flops 2958557184 | bytes 12845056 | tf_op jit(solution)/shard_map/erd,erf->edf/dot_general | solution.py:180
  198.5 7.8 %fusion.2 = bf16[1,2048,704]{1,2,0:T(8,128)(2,1)} fusion(bf16[1024,2048]{1,0:T(8,128)(2,1)} %bitcast.51, f32[1024,704]{0,1:T(8,128)} %fusion.5, f32[1024,704]{0,1:T(8,128)S(1)} %copy-done.11), kind=kOutput, calls=%fused_computation.12 | convolution fusion | flops 2958557184 | bytes 12845056 | tf_op jit(solution)/shard_map/erd,erf->edf/dot_general | solution.py:171
  206.7 3.7 convolution_convert_fusion.4
  212.3 5.3 copy.93
  217.6 3.0 gather_fusion
  220.6 1.6 copy.83
  222.2 5.3 copy.95
  227.5 3.0 gather_fusion.2
  230.5 1.5 copy.78
  232.0 1.9 fusion.55
  235.5 1.0 copy-done.4
  236.9 2.5 copy.70
  239.4 2.8 reshape.548
  242.2 4.3 broadcast_in_dim.38.clone
  246.5 4.5 scatter_fusion
  251.0 6.0 %convert_element_type.125 = bf16[16,128,1024]{2,1,0:T(8,128)(2,1)} convert(f32[16,128,1024]{2,1,0:T(8,128)} %scatter_fusion) | non-fusion elementwise | flops 2097152 | bytes 12582912 | tf_op jit(solution)/shard_map/convert_element_type | solution.py:133
  257.4 1.8 convolution_bitcast_fusion
  259.2 3.1 reshape.556
  262.3 1.9 copy.73
  264.2 4.3 broadcast_in_dim.38.clone.1
  268.5 3.9 scatter_fusion.1
  272.4 6.0 %convert_element_type.128 = bf16[16,128,1024]{2,1,0:T(8,128)(2,1)} convert(f32[16,128,1024]{2,1,0:T(8,128)} %scatter_fusion.1) | non-fusion elementwise | flops 2097152 | bytes 12582912 | tf_op jit(solution)/shard_map/convert_element_type | solution.py:139
  278.5 2.1 fusion.13
  280.6 0.9 copy.76
  281.4 1.9 convert_element_type.137
  283.3 74.9 %reduce-scatter.12.cloned.1.call-done = bf16[1,256,704]{1,2,0:T(8,128)(2,1)} async-done(((bf16[1,2048,704]{1,2,0:T(8,128)(2,1)}), bf16[1,256,704]{1,2,0:T(8,128)(2,1)}) %reduce-scatter.12.cloned.1.call-update) | async-done | bytes 360464 | tf_op jit(solution)/shard_map/reduce_scatter | solution.py:185
  358.2 1.9 convert_element_type.141
  360.1 79.9 %reduce-scatter.14.cloned.1.call-done = bf16[1,256,704]{1,2,0:T(8,128)(2,1)} async-done(((bf16[1,2048,704]{1,2,0:T(8,128)(2,1)}), bf16[1,256,704]{1,2,0:T(8,128)(2,1)}) %reduce-scatter.14.cloned.1.call-update) | async-done | bytes 360464 | tf_op jit(solution)/shard_map/reduce_scatter | solution.py:188
  440.0 1.9 convert_element_type.145
  441.9 68.0 %reduce-scatter.6.cloned.1.call-done = bf16[128,1024]{1,0:T(8,128)(2,1)} async-done(((bf16[2048,1024]{1,0:T(8,128)(2,1)}), bf16[128,1024]{1,0:T(8,128)(2,1)}) %reduce-scatter.6.cloned.1.call-update) | async-done | bytes 262160 | tf_op jit(solution)/shard_map/reduce_scatter | solution.py:132
  510.0 69.8 %reduce-scatter.8.cloned.1.call-done = bf16[128,1024]{1,0:T(8,128)(2,1)} async-done(((bf16[2048,1024]{1,0:T(8,128)(2,1)}), bf16[128,1024]{1,0:T(8,128)(2,1)}) %reduce-scatter.8.cloned.1.call-update) | async-done | bytes 262160 | tf_op jit(solution)/shard_map/reduce_scatter | solution.py:138
  (85 shorter events, 15.5 us)
Async XLA Ops:
  8.0 100.0 %copy-start = (bf16[1,2048,704]{1,2,0:T(8,128)(2,1)S(1)}, bf16[1,2048,704]{1,2,0:T(8,128)(2,1)}, u32[]{:S(2)}) copy-start(bf16[1,2048,704]{1,2,0:T(8,128)(2,1)} %param.23) | copy-start | bytes 8650756
  8.0 204.3 %all-gather.5.cloned.1.call-start = ((), (), s32[]{:S(2)}) async-start(), calls=%async_computation.12 | async-start | bytes 4456448 | tf_op jit(solution)/shard_map/all_gather | solution.py:63
  24.5 7.1 %copy-start.5 = (bf16[1,128,2048]{2,1,0:T(8,128)(2,1)S(1)}, bf16[1,128,2048]{2,1,0:T(8,128)(2,1)}, u32[]{:S(2)}) copy-start(bf16[1,128,2048]{2,1,0:T(8,128)(2,1)} %param.20) | copy-start | bytes 1572868
  24.5 72.1 %all-to-all-start = ((bf16[16,1,64,2048]{3,2,1,0:T(8,128)(2,1)}), bf16[16,1,64,2048]{3,2,1,0:T(8,128)(2,1)}, u32[]{:S(2)}, u32[]{:S(2)}) async-start(bf16[16,1,64,2048]{3,2,1,0:T(8,128)(2,1)} %fusion.25), calls=%async_computation.2 | async-start | bytes 8388608 | tf_op jit(solution)/shard_map/all_to_all | solution.py:156
  30.6 191.6 %all-gather.7.cloned.1.call-start = ((), (), s32[]{:S(2)}) async-start(), calls=%async_computation.13 | async-start | bytes 4456448 | tf_op jit(solution)/shard_map/all_gather | solution.py:64
  96.6 79.5 %all-to-all-start.1 = ((bf16[16,64,2048]{2,1,0:T(8,128)(2,1)}), bf16[16,64,2048]{2,1,0:T(8,128)(2,1)}, u32[]{:S(2)}, u32[]{:S(2)}) async-start(bf16[16,64,2048]{2,1,0:T(8,128)(2,1)} %multiply_convert_fusion), calls=%async_computation.3 | async-start | bytes 8388608 | tf_op jit(solution)/shard_map/all_to_all | solution.py:164
  107.8 173.7 %reduce-scatter.10.cloned.1.call-start = ((), (), s32[]{:S(2)}) async-start(), calls=%async_computation.9 | async-start | bytes 3244032 | tf_op jit(solution)/shard_map/reduce_scatter | solution.py:182
  108.0 7.1 %copy-start.8 = (bf16[1,2048,704]{1,2,0:T(8,128)(2,1)S(1)}, bf16[1,2048,704]{1,2,0:T(8,128)(2,1)}, u32[]{:S(2)}) copy-start(bf16[1,2048,704]{1,2,0:T(8,128)(2,1)} %param.24) | copy-start | bytes 8650756
  115.1 61.0 %copy-start.9 = (bf16[1,2048,704]{1,2,0:T(8,128)(2,1)S(1)}, bf16[1,2048,704]{1,2,0:T(8,128)(2,1)}, u32[]{:S(2)}) copy-start(bf16[1,2048,704]{1,2,0:T(8,128)(2,1)} %param.25) | copy-start | bytes 8650756
  176.1 6.8 %copy-start.10 = (f32[1024,704]{0,1:T(8,128)S(1)}, f32[1024,704]{0,1:T(8,128)}, u32[]{:S(2)}) copy-start(f32[1024,704]{0,1:T(8,128)} %fusion.3) | copy-start | bytes 8650756
  176.1 6.8 %copy-start.12 = (f32[1024,704]{0,1:T(8,128)S(1)}, f32[1024,704]{0,1:T(8,128)}, u32[]{:S(2)}) copy-start(f32[1024,704]{0,1:T(8,128)} %fusion.5) | copy-start | bytes 8650756
  181.3 1.7 copy-start.13
  183.0 7.6 %copy-start.11 = (f32[1024,704]{0,1:T(8,128)S(1)}, f32[1024,704]{0,1:T(8,128)}, u32[]{:S(2)}) copy-start(f32[1024,704]{0,1:T(8,128)} %fusion.3) | copy-start | bytes 8650756
  190.5 167.7 %reduce-scatter.12.cloned.1.call-start = ((), (), s32[]{:S(2)}) async-start(), calls=%async_computation.10 | async-start | bytes 3244032 | tf_op jit(solution)/shard_map/reduce_scatter | solution.py:185
  198.5 241.5 %reduce-scatter.14.cloned.1.call-start = ((), (), s32[]{:S(2)}) async-start(), calls=%async_computation.11 | async-start | bytes 3244032 | tf_op jit(solution)/shard_map/reduce_scatter | solution.py:188
  206.4 4.4 copy-start.6
  206.4 4.4 copy-start.7
  206.4 4.8 copy-start.2
  206.4 303.6 %reduce-scatter.6.cloned.1.call-start = ((), (), s32[]{:S(2)}) async-start(), calls=%async_computation.7 | async-start | bytes 4456448 | tf_op jit(solution)/shard_map/reduce_scatter | solution.py:132
  232.0 2.2 copy-start.3
  235.5 1.0 copy-start.4
  257.1 322.7 %reduce-scatter.8.cloned.1.call-start = ((), (), s32[]{:S(2)}) async-start(), calls=%async_computation.8 | async-start | bytes 4456448 | tf_op jit(solution)/shard_map/reduce_scatter | solution.py:138
  278.4 301.4 %copy-start.1 = (bf16[1,2048,704]{1,2,0:T(8,128)(2,1)S(1)}, bf16[1,2048,704]{1,2,0:T(8,128)(2,1)}, u32[]{:S(2)}) copy-start(bf16[1,2048,704]{1,2,0:T(8,128)(2,1)} %param.23) | copy-start | bytes 8650756
Sparse Core Ops, SparseCore 0:
  10.5 81.3 all-gather.4
  93.6 77.9 all-gather.6
Sparse Core Ops, SparseCore 1:
  190.6 85.7 reduce-scatter.9
  280.1 78.0 reduce-scatter.11
  361.9 78.0 reduce-scatter.13
  443.0 66.9 reduce-scatter.5
  513.0 66.8 reduce-scatter.7
